TPU v7x, 256 devices: a whole 4x4x8 slice. The times are simulated.
256 devices in a mesh: dp: 8 (over z), expert: 8 (over y, core), mp: 4 (over x).
Axes of the slice: x: 4, y: 4, z: 8, core: 2. Of those that a mesh axis runs over, the one named last changes fastest.
Arguments:
- tokens: bfloat16 [8192, 2048], P(('dp', 'expert'), 'mp'), may hold values from -6 to 6
- targets: bfloat16 [8192, 2048], P(('dp', 'expert'), 'mp'), may hold values from -6 to 6
- token_weight: float32 [8192], P(('dp', 'expert')), may hold values from 0.5 to 11.7, as said below
- routes: int32 [8192, 2], P(('dp', 'expert')), may hold values from 0 to 7, all different within a row; in each aligned block of 128 rows (0 to 127, 128 to 255, ...) at most 40 rows name the same one
- router_weight: bfloat16 [2048, 8], P('mp'), may hold values from -0.125 to 0.125
- base_weight: bfloat16 [3, 8, 2048, 8192], P(None, 'expert', None, ('dp', 'mp')), may hold values from -0.125 to 0.125
- direction_one: bfloat16 [3, 8, 2048, 8192], P(None, 'expert', None, ('dp', 'mp')), may hold values from -0.125 to 0.125
- direction_two: bfloat16 [3, 8, 2048, 8192], P(None, 'expert', None, ('dp', 'mp')), may hold values from -0.125 to 0.125
- filter_scale: float32 [2, 8, 8192], P(None, 'expert', ('dp', 'mp')), may hold values from 0.5 to 2
- landscape: float32 [2], replicated, may hold values from -0.6 to 0.6
Outputs:
- mixed: bfloat16 [8192, 2048], P(('dp', 'expert'), 'mp')
- loss: float32 [1], replicated
Inputs may be any that keep to these rules, and one draw needn't show every extreme that they name: `routes`: each row names 2 different experts. Within the rows of one group of dp and expert (aligned blocks of 128 rows) no expert is named more than 40 times, a bound that some block reaches. `token_weight`: Positive.
All inputs are finite; a program needn't handle non-finite values.
Results may differ from a plain program's by a relative error of at most 0.0028.
The roundings to bfloat16 on the way count: a program that leaves them out, or rounds other values in their place, can miss the bound.
Values may be sent and summed in bfloat16 or wider, within the bound.
No kernel may reach another device: no remote copies, remote signals or barrier semaphores. Data moves between devices by JAX's collectives and lax.ppermute only.
A program may use at most 128 MiB of HBM per device.

v0:
```python
import functools

import jax
import jax.numpy as jnp
from jax import lax
from jax.experimental import pallas as pl
from jax.experimental.pallas import tpu as pltpu
from jax.sharding import Mesh
from jax.sharding import PartitionSpec as P

CAP = 40
MP = 4
EXPERT = ("expert_0", "expert_1")
DP_EXPERT = ("dp", "expert_0", "expert_1")
F32 = jnp.float32
BF16 = jnp.bfloat16
WIRE = jnp.float16


def shifted(array, axis, step):
    count = lax.axis_size(axis)
    return lax.ppermute(array, axis, [(i, (i + step) % count) for i in range(count)])


def to_all(array, axes):
    count = lax.axis_size(axes)
    copies = jnp.broadcast_to(array, (count, *array.shape))
    copies = lax.all_to_all(copies, axes, split_axis=0, concat_axis=0, tiled=True)
    return copies.reshape(count, *array.shape)


def hidden_of(slots, rows, weights):
    hidden = []
    for gate, up, _ in weights:
        gate_value = jnp.dot(slots[rows, :], gate[...], preferred_element_type=F32)
        up_value = jnp.dot(slots[rows, :], up[...], preferred_element_type=F32)
        hidden.append((gate_value / (1.0 + jnp.exp(-gate_value)) * up_value).astype(BF16))
    return hidden


def output_of(value, hidden, weights, width, start, span):
    for values, (_, _, downs) in zip(hidden, weights):
        depth = width // len(downs)
        down = downs[start // depth]
        first = start % depth
        added = lax.dot_general(
            values, down[first : first + span, :], (((1,), (1,)), ((), ())),
            preferred_element_type=F32,
        )
        value = added if value is None else value + added
    return value


def first_kernel(skips, index_ref, *refs):
    count = len(skips)
    blocks, (gate, up, down, slots, total) = refs[:count], refs[count:]
    feat = slots.shape[1] // MP
    index = index_ref[0]
    row = 0
    for block, skip in zip(blocks, skips):
        rows = block.shape[0] - skip
        for step in range(MP):
            source = lax.rem(index + MP - step, MP)
            columns = pl.ds(pl.multiple_of(source * feat, feat), feat)
            slots[row : row + rows, columns] = block[skip:, step * feat : (step + 1) * feat]
        row += rows
    pass_through(slots, None, total, [(gate, up, (down,))])


def pass_through(slots, before, total, weights):
    height, width = slots.shape
    chunk = height // 2
    span = 512

    @pl.loop(0, 2)
    def _(turn):
        rows = pl.ds(pl.multiple_of(turn * chunk, chunk), chunk)
        hidden = hidden_of(slots, rows, weights)
        for start in range(0, width, span):
            cut = slice(start, start + span)
            value = None if before is None else before[rows, cut]
            total[rows, cut] = output_of(value, hidden, weights, width, start, span)


def middle_kernel(slots, before, *refs):
    weights, total = refs[:-1], refs[-1]
    sets = [(weights[i], weights[i + 1], weights[i + 2 : i + 3]) for i in range(0, len(weights), 3)]
    pass_through(slots, before, total, sets)


def last_kernel(slots, before, gate, up, low, high, *outs):
    height, width = slots.shape
    chunk = height // 2
    span = 512
    weights = [(gate, up, (low, high))]
    for turn in (1, 0):
        rows = slice(turn * chunk, (turn + 1) * chunk)
        hidden = hidden_of(slots, rows, weights)
        for start in range(0, width, span):
            cut = slice(start, start + span)
            value = output_of(before[rows, cut], hidden, weights, width, start, span)
            row = 0
            for out in outs:
                size = out.shape[0]
                if turn * chunk <= row < (turn + 1) * chunk:
                    at = row - turn * chunk
                    out[:, cut] = value[at : at + size]
                row += size


def expert_call(kernel, args, out_shape, rows, width, hidden, scalars):
    whole = pl.BlockSpec(memory_space=pltpu.VMEM)
    single = isinstance(out_shape, jax.ShapeDtypeStruct)
    return pl.pallas_call(
        kernel,
        out_shape=out_shape,
        in_specs=[pl.BlockSpec(memory_space=pltpu.SMEM)] * scalars + [whole] * (len(args) - scalars),
        out_specs=whole if single else [whole] * len(out_shape),
        compiler_params=pltpu.CompilerParams(vmem_limit_bytes=44 * 1024 * 1024),
        cost_estimate=pl.CostEstimate(
            flops=6 * rows * width * hidden,
            bytes_accessed=6 * width * hidden + 8 * rows * width,
            transcendentals=rows * hidden,
        ),
    )(*args)


def rebuild(base_weight, direction_one, direction_two, filter_scale, landscape):
    scale_one = filter_scale[0][None, :]
    scale_two = filter_scale[1][None, :]
    merged = (
        base_weight.astype(F32)
        + landscape[0] * scale_one * direction_one.astype(F32)
        + landscape[1] * scale_two * direction_two.astype(F32)
    )
    return merged.astype(BF16)


def rebuild_kernel(landscape_ref, base_ref, one_ref, two_ref, scale_ref, out_ref):
    scale_one = landscape_ref[0] * scale_ref[0]
    scale_two = landscape_ref[1] * scale_ref[1]
    merged = (
        base_ref[0, 0].astype(F32)
        + scale_one * one_ref[0, 0].astype(F32)
        + scale_two * two_ref[0, 0].astype(F32)
    )
    out_ref[...] = merged.astype(BF16)


def rebuild_call(matrix, base_weight, direction_one, direction_two, filter_scale, landscape):
    _, _, width, hidden = base_weight.shape
    rows = width // 4
    block = pl.BlockSpec((1, 1, rows, hidden), lambda i: (matrix, 0, i, 0))
    return pl.pallas_call(
        rebuild_kernel,
        grid=(width // rows,),
        out_shape=jax.ShapeDtypeStruct((width, hidden), BF16),
        in_specs=[
            pl.BlockSpec(memory_space=pltpu.SMEM),
            block,
            block,
            block,
            pl.BlockSpec(filter_scale.shape, lambda i: (0, 0, 0)),
        ],
        out_specs=pl.BlockSpec((rows, hidden), lambda i: (i, 0)),
        compiler_params=pltpu.CompilerParams(vmem_limit_bytes=62 * 1024 * 1024),
        cost_estimate=pl.CostEstimate(
            flops=4 * width * hidden, bytes_accessed=8 * width * hidden, transcendentals=0
        ),
    )(landscape, base_weight, direction_one, direction_two, filter_scale)


def slot_target(routes, expert_count, capacity):
    pair_ids = jnp.concatenate([routes[:, 0], routes[:, 1]])
    expert_ids = jnp.arange(expert_count, dtype=jnp.int32)
    onehot = (pair_ids[:, None] == expert_ids[None, :]).astype(jnp.int32)
    earlier = jnp.cumsum(onehot, axis=0) - onehot
    slot = jnp.sum(earlier * onehot, axis=1)
    return pair_ids * capacity + slot


def per_device(
    tokens,
    targets,
    token_weight,
    routes,
    router_weight,
    base_weight,
    direction_one,
    direction_two,
    filter_scale,
    landscape,
):
    tok_rows, feat = tokens.shape
    expert_count = router_weight.shape[1]
    width = base_weight.shape[2]
    own_hidden = base_weight.shape[3]
    dp_count = lax.axis_size("dp")
    mp_count = lax.axis_size("mp")
    mp_index = lax.axis_index("mp")

    def rebuilt(m, scale):
        return rebuild(base_weight[m, 0], direction_one[m, 0], direction_two[m, 0], scale[:, 0], landscape)

    gate_own = rebuild_call(0, base_weight, direction_one, direction_two, filter_scale, landscape)
    gate_left = shifted(gate_own, "mp", 1)
    gate_right = shifted(gate_own, "mp", -1)
    tokens_then, _ = lax.optimization_barrier((tokens, gate_own))

    flat_index = slot_target(routes, expert_count, CAP)
    placer = (
        flat_index[:, None] == jnp.arange(expert_count * CAP, dtype=jnp.int32)[None, :]
    ).astype(BF16)
    doubled = jnp.concatenate([tokens_then, tokens_then], axis=0)
    buffer = jnp.einsum("pk,pf->kf", placer, doubled, preferred_element_type=F32).astype(BF16)
    buffer = buffer.reshape(expert_count, CAP, feat)
    received = lax.all_to_all(buffer, EXPERT, split_axis=0, concat_axis=0, tiled=True)
    quarters = received.reshape(mp_count, (expert_count // mp_count) * CAP, feat)
    rows = quarters.shape[1]
    part = rows // 2

    scale_then, _ = lax.optimization_barrier((filter_scale, buffer))
    up_own, down_own = rebuilt(1, scale_then), rebuilt(2, scale_then)

    partial_logits = lax.dot_general(
        router_weight, tokens, (((0,), (1,)), ((), ())), preferred_element_type=F32
    )
    high = lax.reduce_precision(partial_logits, 8, 7)
    middle = lax.reduce_precision(partial_logits - high, 8, 7)
    low = partial_logits - high - middle
    wide = [matrix.astype(F32) for matrix in (gate_own, up_own, down_own)]
    energy = jnp.sum(jnp.sum(wide[0] ** 2, axis=0) * jnp.sum(wide[1] ** 2, axis=0))
    reach = jnp.max(jnp.sum(wide[2] ** 2, axis=1))
    longest = jnp.max(jnp.sum(received.astype(F32) ** 2, axis=2))
    kind = lax.broadcasted_iota(jnp.int32, high.shape, 0)
    limits = 1.02 * jnp.where(kind == 0, energy, jnp.where(kind == 1, reach, longest))
    extra = jnp.concatenate([high, middle, low, limits], axis=1).astype(BF16)
    head = extra.shape[0]

    pieces = []
    for step in range(mp_count):
        target = lax.rem(mp_index + step, mp_count)
        piece = lax.dynamic_index_in_dim(quarters, target, 0, keepdims=False)
        piece = jnp.concatenate([extra, piece], axis=0)
        pieces.append(shifted(piece, "mp", step) if step else piece)
    slots = jnp.concatenate(pieces, axis=1)

    up_then, down_then, _ = lax.optimization_barrier((up_own, down_own, received))
    up_left = shifted(up_then, "mp", 1)
    up_right = shifted(up_then, "mp", -1)
    down_left = shifted(down_then, "mp", 1)
    down_right = shifted(down_then, "mp", -1)
    gate_far = shifted(gate_left, "mp", 1)
    up_far = shifted(up_right, "mp", -1)

    forward = [slots]
    backward = [slots]
    for _ in range(1, dp_count // 2):
        forward.append(shifted(forward[-1], "dp", 1))
        backward.append(shifted(backward[-1], "dp", -1))
    far_low = shifted(forward[-1][: head + part], "dp", 1)
    far_high = shifted(backward[-1][head + part :], "dp", -1)

    middle_row = width // 2
    first_half, second_half, _, _ = lax.optimization_barrier((down_left, down_right, far_low, far_high))
    down_far = (
        shifted(first_half[:middle_row], "mp", 1), shifted(second_half[middle_row:], "mp", -1)
    )

    heads = [block[:head] for block in forward + backward[1:] + [far_low]]
    limits = functools.reduce(jnp.maximum, [block.astype(F32) for block in heads])
    limits = jnp.max(limits.reshape(head, mp_count, feat)[:, :, feat - tok_rows :], axis=(1, 2))
    devices = float(dp_count * mp_count)
    bound = 1.1 * devices * mp_count * limits[2] * jnp.sqrt(limits[0]) * jnp.sqrt(limits[1])
    bound = jnp.maximum(bound, 1e-20)
    to_wire = 32768.0 / bound
    from_wire = bound * (1.0 / 32768.0)

    parts = slots[:head].astype(F32).reshape(head, mp_count, 4, tok_rows)[:, :, :3]
    logits = jnp.sum(parts, axis=(1, 2))

    blocks = [slots]
    for ahead, behind in zip(forward[1:], backward[1:]):
        blocks += [ahead, behind]
    blocks += [far_low, far_high]
    skips = (head,) * (len(blocks) - 1) + (0,)
    all_rows = dp_count * rows
    slots_shape = jax.ShapeDtypeStruct((all_rows, width), BF16)
    total_shape = jax.ShapeDtypeStruct((all_rows, width), F32)
    place = mp_index.astype(jnp.int32).reshape(1)
    every, sums = expert_call(
        functools.partial(first_kernel, skips),
        (place, *blocks, gate_own, up_own, down_own),
        [slots_shape, total_shape], all_rows, width, own_hidden, 1,
    )
    sums = expert_call(
        middle_kernel,
        (every, sums, gate_left, up_left, down_left, gate_right, up_right, down_right),
        total_shape, all_rows, width, 2 * own_hidden, 0,
    )
    heights = [rows] * (dp_count - 1) + [part, part]
    outs = expert_call(
        last_kernel,
        (every, sums, gate_far, up_far, *down_far),
        [jax.ShapeDtypeStruct((height, width), F32) for height in heights],
        all_rows, width, own_hidden, 0,
    )
    outs = [out * to_wire for out in outs]

    def both(below, above):
        pair = lax.optimization_barrier((below.astype(WIRE), above.astype(WIRE)))
        pair = lax.optimization_barrier((shifted(pair[0], "dp", -1), shifted(pair[1], "dp", 1)))
        return pair[0].astype(F32), pair[1].astype(F32)

    back, ahead = both(outs[-2], outs[-1])
    below, above = outs[-4], outs[-3]
    below = jnp.concatenate([below[:part] + back, below[part:]], axis=0)
    above = jnp.concatenate([above[:part], above[part:] + ahead], axis=0)
    back, ahead = both(below, above)
    for step in range(dp_count // 2 - 2, 0, -1):
        back, ahead = both(outs[2 * step - 1] + back, outs[2 * step] + ahead)
    result = ((outs[0] + back + ahead) * from_wire).astype(BF16)

    arrived = []
    for step in range(mp_count):
        target = lax.rem(mp_index + step, mp_count)
        piece = lax.dynamic_slice(result, (0, target * feat), (rows, feat))
        arrived.append(shifted(piece, "mp", step) if step else piece)

    def quarter(place):
        step = lax.rem(mp_index - place + mp_count, mp_count)
        chosen = arrived[-1]
        for i, piece in enumerate(arrived[:-1]):
            chosen = jnp.where(step == i, piece, chosen)
        return chosen

    expert_out = jnp.stack([quarter(i) for i in range(mp_count)]).reshape(expert_count, CAP, feat)
    returned = lax.all_to_all(expert_out, EXPERT, split_axis=0, concat_axis=0, tiled=True)

    expert_ids = jnp.arange(expert_count, dtype=jnp.int32)
    pick_first = jnp.sum(jnp.where(routes[:, 0][None, :] == expert_ids[:, None], logits, 0.0), axis=0)
    pick_second = jnp.sum(jnp.where(routes[:, 1][None, :] == expert_ids[:, None], logits, 0.0), axis=0)
    gate_first = 1.0 / (1.0 + jnp.exp(pick_second - pick_first))
    gate_second = 1.0 / (1.0 + jnp.exp(pick_first - pick_second))

    out_rows = returned.reshape(expert_count * CAP, feat)
    picked = jnp.dot(placer, out_rows, preferred_element_type=F32)
    first_out, second_out = picked[:tok_rows], picked[tok_rows:]
    combined = (
        tokens.astype(F32) + gate_first[:, None] * first_out + gate_second[:, None] * second_out
    )
    error = combined - targets.astype(F32)
    partial_loss = jnp.sum(token_weight[:, None] * error * error)
    loss_total = jnp.sum(to_all(partial_loss.reshape(1, 1), ("dp", "expert_0", "expert_1", "mp")))
    entries = tok_rows * dp_count * expert_count * feat * mp_count
    loss = (loss_total / entries).reshape(1)
    return (combined.astype(BF16), loss)


def solution(mesh):
    split = Mesh(
        mesh.devices.reshape(mesh.shape["dp"], 4, 2, mesh.shape["mp"]),
        ("dp", "expert_0", "expert_1", "mp"),
    )

    return jax.shard_map(
        per_device,
        mesh=split,
        in_specs=(
            P(DP_EXPERT, "mp"),
            P(DP_EXPERT, "mp"),
            P(DP_EXPERT),
            P(DP_EXPERT, None),
            P("mp", None),
            P(None, EXPERT, None, ("dp", "mp")),
            P(None, EXPERT, None, ("dp", "mp")),
            P(None, EXPERT, None, ("dp", "mp")),
            P(None, EXPERT, ("dp", "mp")),
            P(),
        ),
        out_specs=(P(DP_EXPERT, "mp"), P()),
        check_vma=False,
    )
```

profile of v0, /device:TPU:2, one launch (start us, length us, event | category | flops | bytes accessed | tf_op | source)
XLA Modules:
  0.0 241.5 jit_solution(15432310373917800936)
XLA Ops:
  2.4 4.0 %shard_map.113.refs_9_ = bf16[2048,256]{1,0:T(8,128)(2,1)} custom-call(f32[2]{0:T(128)} %landscape_ref.1, bf16[3,1,2048,256]{3,2,1,0:T(8,128)(2,1)} %base_ref.1, bf16[3,1,2048,256]{3,2,1,0:T(8,128)(2,1)} %one_ref.1, bf16[3,1,2048,256]{3,2,1,0:T(8,128)(2,1)} %two_ref.1, f32[2,1,256]{2,1,0:T(1,128)} %scale_ref.1), custom_call_target="tpu_custom_call" | custom-call | flops 2097152 | bytes 4194304 | tf_op jit(solution)/shard_map/pallas_call | solution.py:154
  7.5 4.5 %all-to-all-start = ((bf16[8,40,512]{2,1,0:T(8,128)(2,1)}), bf16[8,40,512]{2,1,0:T(8,128)(2,1)S(1)}, u32[]{:S(2)}, u32[]{:S(2)}) async-start(bf16[8,40,512]{2,1,0:T(8,128)(2,1)} %bitcast.7), calls=%async_computation | async-start | bytes 655360 | tf_op jit(solution)/shard_map/all_to_all | solution.py:217
  14.3 3.5 %multiply_reduce_fusion.1 = (f32[256]{0:T(256)S(1)}, bf16[2048,256]{1,0:T(8,128)(2,1)S(1)}, f32[2048]{0:T(1024)S(1)}, bf16[2048,256]{1,0:T(8,128)(2,1)S(1)}) fusion(bf16[3,1,2048,256]{3,2,1,0:T(8,128)(2,1)} %two_ref.1, f32[256]{0:T(256)S(1)} %bitcast.76, bf16[3,1,2048,256]{3,2,1,0:T(8,128)(2,1)} %one_ref.1, f32[256]{0:T(256)S(1)} %bitcast.75, ...), kind=kLoop, calls=%fused_computation.11 | loop fusion | flops 11532032 | bytes 8399872 | tf_op jit(solution)/shard_map/reduce_sum | solution.py:232
  33.9 4.0 %collective-permute-start.4 = (bf16[88,2048]{1,0:T(8,128)(2,1)S(1)}, bf16[88,2048]{1,0:T(8,128)(2,1)S(1)}, u32[]{:S(2)}, u32[]{:S(2)}) collective-permute-start(bf16[88,2048]{1,0:T(8,128)(2,1)S(1)} %pad_maximum_fusion.refs_0_), channel_id=1, source_target_pairs={{0,224},{32,0},{64,32},{96,64},{128,96},{160,128},{192,160},{224,1... | collective-permute-start | bytes 1081352 | tf_op jit(solution)/shard_map/ppermute | solution.py:22
  39.2 6.1 %collective-permute-done.3.refs_1_ = bf16[88,2048]{1,0:T(8,128)(2,1)S(1)} collective-permute-done((bf16[88,2048]{1,0:T(8,128)(2,1)S(1)}, bf16[88,2048]{1,0:T(8,128)(2,1)S(1)}, u32[]{:S(2)}, u32[]{:S(2)}) %collective-permute-start.3) | collective-permute-done | bytes 360480 | tf_op jit(solution)/shard_map/ppermute | solution.py:22
  49.8 5.3 %collective-permute-done.5.refs_3_ = bf16[88,2048]{1,0:T(8,128)(2,1)S(1)} collective-permute-done((bf16[88,2048]{1,0:T(8,128)(2,1)S(1)}, bf16[88,2048]{1,0:T(8,128)(2,1)S(1)}, u32[]{:S(2)}, u32[]{:S(2)}) %collective-permute-start.5) | collective-permute-done | bytes 360480 | tf_op jit(solution)/shard_map/ppermute | solution.py:22
  56.5 5.9 %collective-permute-start.8 = (bf16[88,2048]{1,0:T(8,128)(2,1)S(1)}, bf16[88,2048]{1,0:T(8,128)(2,1)S(1)}, u32[]{:S(2)}, u32[]{:S(2)}) collective-permute-start(bf16[88,2048]{1,0:T(8,128)(2,1)S(1)} %collective-permute-done.6.refs_4_), channel_id=1, source_target_pairs={{0,224},{32,0},{64,32},{96,64},{128,96},{160,128},{192,160},{224,1... | collective-permute-start | bytes 1081352 | tf_op jit(solution)/shard_map/ppermute | solution.py:22
  65.4 9.9 %collective-permute-done.13.refs_2_ = bf16[2048,256]{1,0:T(8,128)(2,1)S(1)} collective-permute-done((bf16[2048,256]{1,0:T(8,128)(2,1)S(1)}, bf16[2048,256]{1,0:T(8,128)(2,1)S(1)}, u32[]{:S(2)}, u32[]{:S(2)}) %collective-permute-start.13) | collective-permute-done | bytes 1048608 | tf_op jit(solution)/shard_map/ppermute | solution.py:22
  79.5 5.8 %collective-permute-done.9.refs_7_ = bf16[48,2048]{1,0:T(8,128)(2,1)S(1)} collective-permute-done((bf16[48,2048]{1,0:T(8,128)(2,1)S(1)}, bf16[48,2048]{1,0:T(8,128)(2,1)S(1)}, u32[]{:S(2)}, u32[]{:S(2)}) %collective-permute-start.9) | collective-permute-done | bytes 196640 | tf_op jit(solution)/shard_map/ppermute | solution.py:22
  87.7 6.1 %collective-permute-done.16.refs_5_ = bf16[2048,256]{1,0:T(8,128)(2,1)S(1)} collective-permute-done((bf16[2048,256]{1,0:T(8,128)(2,1)S(1)}, bf16[2048,256]{1,0:T(8,128)(2,1)S(1)}, u32[]{:S(2)}, u32[]{:S(2)}) %collective-permute-start.16) | collective-permute-done | bytes 1048608 | tf_op jit(solution)/shard_map/ppermute | solution.py:22
  102.3 14.0 %collective-permute-done.14.refs_3_ = bf16[2048,256]{1,0:T(8,128)(2,1)S(1)} collective-permute-done((bf16[2048,256]{1,0:T(8,128)(2,1)S(1)}, bf16[2048,256]{1,0:T(8,128)(2,1)S(1)}, u32[]{:S(2)}, u32[]{:S(2)}) %collective-permute-start.14) | collective-permute-done | bytes 1048608 | tf_op jit(solution)/shard_map/ppermute | solution.py:22
  117.6 5.0 %shard_map.114 = (bf16[640,2048]{1,0:T(8,128)(2,1)S(1)}, f32[640,2048]{1,0:T(8,128)}) custom-call(s32[1]{0:T(128)} %bitcast.22.index_ref, bf16[88,2048]{1,0:T(8,128)(2,1)S(1)} %pad_maximum_fusion.refs_0_, bf16[88,2048]{1,0:T(8,128)(2,1)S(1)} %collective-permute-done.3.refs_1_, bf16[88,2048]{1,0:T(8,128)(2,1)S(1)} %collective-permute-done.4.refs_2_, ...), custom_call_target="tpu_custom_call" | custom-call | flops 2013265920 | bytes 13631488 | tf_op jit(solution)/shard_map/pallas_call | solution.py:114
  122.6 10.3 %shard_map.115.before = f32[640,2048]{1,0:T(8,128)} custom-call(bf16[640,2048]{1,0:T(8,128)(2,1)S(1)} %get-tuple-element.37.slots, f32[640,2048]{1,0:T(8,128)} %get-tuple-element.38.before, bf16[2048,256]{1,0:T(8,128)(2,1)S(1)} %collective-permute-done.11.refs_0_, bf16[2048,256]{1,0:T(8,128)(2,1)S(1)} %collective-permute-done.12.refs_1_, ...), custom_call_target="tpu_custom_call" | custom-call | flops 4026531840 | bytes 16777216 | tf_op jit(solution)/shard_map/pallas_call | solution.py:114
  135.4 12.1 %collective-permute-done.20.high = bf16[1024,256]{1,0:T(8,128)(2,1)S(1)} collective-permute-done((bf16[1024,256]{1,0:T(8,128)(2,1)S(1)}, bf16[1024,256]{1,0:T(8,128)(2,1)S(1)}, u32[]{:S(2)}, u32[]{:S(2)}) %collective-permute-start.20) | collective-permute-done | bytes 524320 | tf_op jit(solution)/shard_map/ppermute | solution.py:22
  147.5 5.8 %shard_map.116 = (f32[80,2048]{1,0:T(8,128)S(1)}, f32[80,2048]{1,0:T(8,128)S(1)}, f32[80,2048]{1,0:T(8,128)S(1)}, f32[80,2048]{1,0:T(8,128)S(1)}, f32[80,2048]{1...) custom-call(bf16[640,2048]{1,0:T(8,128)(2,1)} %copy-done.1, ...), custom_call_target="tpu_custom_call" | custom-call | flops 2013265920 | bytes 13631488 | tf_op jit(solution)/shard_map/pallas_call | solution.py:114
  159.3 3.7 %collective-permute-done.22 = f16[40,2048]{1,0:T(8,128)(2,1)S(1)} collective-permute-done((f16[40,2048]{1,0:T(8,128)(2,1)S(1)}, f16[40,2048]{1,0:T(8,128)(2,1)S(1)}, u32[]{:S(2)}, u32[]{:S(2)}) %collective-permute-start.22) | collective-permute-done | bytes 163872 | tf_op jit(solution)/shard_map/ppermute | solution.py:22
  165.4 6.1 %collective-permute-done.23 = f16[80,2048]{1,0:T(8,128)(2,1)S(1)} collective-permute-done((f16[80,2048]{1,0:T(8,128)(2,1)S(1)}, f16[80,2048]{1,0:T(8,128)(2,1)S(1)}, u32[]{:S(2)}, u32[]{:S(2)}) %collective-permute-start.23) | collective-permute-done | bytes 327712 | tf_op jit(solution)/shard_map/ppermute | solution.py:22
  175.1 6.1 %collective-permute-done.25 = f16[80,2048]{1,0:T(8,128)(2,1)S(1)} collective-permute-done((f16[80,2048]{1,0:T(8,128)(2,1)S(1)}, f16[80,2048]{1,0:T(8,128)(2,1)S(1)}, u32[]{:S(2)}, u32[]{:S(2)}) %collective-permute-start.25) | collective-permute-done | bytes 327712 | tf_op jit(solution)/shard_map/ppermute | solution.py:22
  186.2 4.9 %collective-permute-done.27 = f16[80,2048]{1,0:T(8,128)(2,1)S(1)} collective-permute-done((f16[80,2048]{1,0:T(8,128)(2,1)S(1)}, f16[80,2048]{1,0:T(8,128)(2,1)S(1)}, u32[]{:S(2)}, u32[]{:S(2)}) %collective-permute-start.27) | collective-permute-done | bytes 327712 | tf_op jit(solution)/shard_map/ppermute | solution.py:22
  191.1 3.4 %collective-permute-done.28 = f16[80,2048]{1,0:T(8,128)(2,1)S(1)} collective-permute-done((f16[80,2048]{1,0:T(8,128)(2,1)S(1)}, f16[80,2048]{1,0:T(8,128)(2,1)S(1)}, u32[]{:S(2)}, u32[]{:S(2)}) %collective-permute-start.28) | collective-permute-done | bytes 327712 | tf_op jit(solution)/shard_map/ppermute | solution.py:22
  194.7 3.8 %collective-permute-start.29 = (bf16[80,512]{1,0:T(8,128)(2,1)S(1)}, bf16[80,512]{1,0:T(8,128)(2,1)S(1)}, u32[]{:S(2)}, u32[]{:S(2)}) collective-permute-start(bf16[80,512]{1,0:T(8,128)(2,1)S(1)} %get-tuple-element.88), channel_id=1, source_target_pairs={{0,2},{1,3},{2,0},{3,1},{4,6},{5,7},{6,4},{7,5},{8,10},{9,11},{10,... | collective-permute-start | bytes 245768 | tf_op jit(solution)/shard_map/ppermute | solution.py:22
  203.7 4.7 %all-to-all-start.1 = ((bf16[8,40,512]{2,1,0:T(8,128)(2,1)}), bf16[8,40,512]{2,1,0:T(8,128)(2,1)S(1)}, u32[]{:S(2)}, u32[]{:S(2)}) async-start(bf16[8,40,512]{2,1,0:T(8,128)(2,1)} %bitcast.30), calls=%async_computation.1 | async-start | bytes 655360 | tf_op jit(solution)/shard_map/all_to_all | solution.py:338
  208.5 8.2 %all-to-all-done.1 = bf16[8,40,512]{2,1,0:T(8,128)(2,1)S(1)} async-done(((bf16[8,40,512]{2,1,0:T(8,128)(2,1)}), bf16[8,40,512]{2,1,0:T(8,128)(2,1)S(1)}, u32[]{:S(2)}, u32[]{:S(2)}) %all-to-all-start.1) | async-done | bytes 327712 | tf_op jit(solution)/shard_map/all_to_all | solution.py:338
  219.2 19.7 %all_to_all.15 = f32[256,1,1]{2,1,0:T(1,128)S(1)} all-to-all(f32[256,1,1]{2,1,0:T(1,128)S(1)} %broadcast_in_dim.33), channel_id=1, replica_groups=mesh['dp'=8,'expert_0'=4,'expert_1'=2,'mp'=4] {'dp','expert_0','expert_1..., dimensions={0} | all-to-all | bytes 2048 | tf_op jit(solution)/shard_map/all_to_all | solution.py:28
  (122 shorter events, 74.0 us)
Async XLA Ops:
  7.5 12.7 %all-to-all-start = ((bf16[8,40,512]{2,1,0:T(8,128)(2,1)}), bf16[8,40,512]{2,1,0:T(8,128)(2,1)S(1)}, u32[]{:S(2)}, u32[]{:S(2)}) async-start(bf16[8,40,512]{2,1,0:T(8,128)(2,1)} %bitcast.7), calls=%async_computation | async-start | bytes 655360 | tf_op jit(solution)/shard_map/all_to_all | solution.py:217
  27.8 27.4 %collective-permute-start.11 = (bf16[2048,256]{1,0:T(8,128)(2,1)S(1)}, bf16[2048,256]{1,0:T(8,128)(2,1)S(1)}, u32[]{:S(2)}, u32[]{:S(2)}) collective-permute-start(bf16[2048,256]{1,0:T(8,128)(2,1)S(1)} %copy-done.2), channel_id=1, source_target_pairs={{0,1},{1,2},{2,3},{3,0},{4,5},{5,6},{6,7},{7,4},{8,9},{9,10},{10,1... | collective-permute-start | bytes 3145736 | tf_op jit(solution)/shard_map/ppermute | solution.py:22
  32.5 12.8 %collective-permute-start.3 = (bf16[88,2048]{1,0:T(8,128)(2,1)S(1)}, bf16[88,2048]{1,0:T(8,128)(2,1)S(1)}, u32[]{:S(2)}, u32[]{:S(2)}) collective-permute-start(bf16[88,2048]{1,0:T(8,128)(2,1)S(1)} %pad_maximum_fusion.refs_0_), channel_id=1, source_target_pairs={{0,32},{32,64},{64,96},{96,128},{128,160},{160,192},{192,224},{224... | collective-permute-start | bytes 1081352 | tf_op jit(solution)/shard_map/ppermute | solution.py:22
  33.9 12.7 %collective-permute-start.4 = (bf16[88,2048]{1,0:T(8,128)(2,1)S(1)}, bf16[88,2048]{1,0:T(8,128)(2,1)S(1)}, u32[]{:S(2)}, u32[]{:S(2)}) collective-permute-start(bf16[88,2048]{1,0:T(8,128)(2,1)S(1)} %pad_maximum_fusion.refs_0_), channel_id=1, source_target_pairs={{0,224},{32,0},{64,32},{96,64},{128,96},{160,128},{192,160},{224,1... | collective-permute-start | bytes 1081352 | tf_op jit(solution)/shard_map/ppermute | solution.py:22
  37.9 37.4 %collective-permute-start.13 = (bf16[2048,256]{1,0:T(8,128)(2,1)S(1)}, bf16[2048,256]{1,0:T(8,128)(2,1)S(1)}, u32[]{:S(2)}, u32[]{:S(2)}) collective-permute-start(bf16[2048,256]{1,0:T(8,128)(2,1)S(1)} %get-tuple-element.40.refs_11_), channel_id=1, source_target_pairs={{0,1},{1,2},{2,3},{3,0},{4,5},{5,6},{6,7},{7,4},{8,9},{9,10},{10,1... | collective-permute-start | bytes 3145736 | tf_op jit(solution)/shard_map/ppermute | solution.py:22
  45.3 9.8 %collective-permute-start.5 = (bf16[88,2048]{1,0:T(8,128)(2,1)S(1)}, bf16[88,2048]{1,0:T(8,128)(2,1)S(1)}, u32[]{:S(2)}, u32[]{:S(2)}) collective-permute-start(bf16[88,2048]{1,0:T(8,128)(2,1)S(1)} %collective-permute-done.3.refs_1_), channel_id=1, source_target_pairs={{0,32},{32,64},{64,96},{96,128},{128,160},{160,192},{192,224},{224... | collective-permute-start | bytes 1081352 | tf_op jit(solution)/shard_map/ppermute | solution.py:22
  45.3 33.4 %collective-permute-start.15 = (bf16[2048,256]{1,0:T(8,128)(2,1)S(1)}, bf16[2048,256]{1,0:T(8,128)(2,1)S(1)}, u32[]{:S(2)}, u32[]{:S(2)}) collective-permute-start(bf16[2048,256]{1,0:T(8,128)(2,1)S(1)} %get-tuple-element.39.refs_10_), channel_id=1, source_target_pairs={{0,3},{1,0},{2,1},{3,2},{4,7},{5,4},{6,5},{7,6},{8,11},{9,8},{10,9... | collective-permute-start | bytes 3145736 | tf_op jit(solution)/shard_map/ppermute | solution.py:22
  46.6 9.8 %collective-permute-start.6 = (bf16[88,2048]{1,0:T(8,128)(2,1)S(1)}, bf16[88,2048]{1,0:T(8,128)(2,1)S(1)}, u32[]{:S(2)}, u32[]{:S(2)}) collective-permute-start(bf16[88,2048]{1,0:T(8,128)(2,1)S(1)} %collective-permute-done.4.refs_2_), channel_id=1, source_target_pairs={{0,224},{32,0},{64,32},{96,64},{128,96},{160,128},{192,160},{224,1... | collective-permute-start | bytes 1081352 | tf_op jit(solution)/shard_map/ppermute | solution.py:22
  55.2 9.0 %collective-permute-start.7 = (bf16[88,2048]{1,0:T(8,128)(2,1)S(1)}, bf16[88,2048]{1,0:T(8,128)(2,1)S(1)}, u32[]{:S(2)}, u32[]{:S(2)}) collective-permute-start(bf16[88,2048]{1,0:T(8,128)(2,1)S(1)} %collective-permute-done.5.refs_3_), channel_id=1, source_target_pairs={{0,32},{32,64},{64,96},{96,128},{128,160},{160,192},{192,224},{224... | collective-permute-start | bytes 1081352 | tf_op jit(solution)/shard_map/ppermute | solution.py:22
  55.2 38.6 %collective-permute-start.16 = (bf16[2048,256]{1,0:T(8,128)(2,1)S(1)}, bf16[2048,256]{1,0:T(8,128)(2,1)S(1)}, u32[]{:S(2)}, u32[]{:S(2)}) collective-permute-start(bf16[2048,256]{1,0:T(8,128)(2,1)S(1)} %get-tuple-element.40.refs_11_), channel_id=1, source_target_pairs={{0,3},{1,0},{2,1},{3,2},{4,7},{5,4},{6,5},{7,6},{8,11},{9,8},{10,9... | collective-permute-start | bytes 3145736 | tf_op jit(solution)/shard_map/ppermute | solution.py:22
  56.5 20.8 %collective-permute-start.8 = (bf16[88,2048]{1,0:T(8,128)(2,1)S(1)}, bf16[88,2048]{1,0:T(8,128)(2,1)S(1)}, u32[]{:S(2)}, u32[]{:S(2)}) collective-permute-start(bf16[88,2048]{1,0:T(8,128)(2,1)S(1)} %collective-permute-done.6.refs_4_), channel_id=1, source_target_pairs={{0,224},{32,0},{64,32},{96,64},{128,96},{160,128},{192,160},{224,1... | collective-permute-start | bytes 1081352 | tf_op jit(solution)/shard_map/ppermute | solution.py:22
  64.2 52.1 %collective-permute-start.14 = (bf16[2048,256]{1,0:T(8,128)(2,1)S(1)}, bf16[2048,256]{1,0:T(8,128)(2,1)S(1)}, u32[]{:S(2)}, u32[]{:S(2)}) collective-permute-start(bf16[2048,256]{1,0:T(8,128)(2,1)S(1)} %copy-done.2), channel_id=1, source_target_pairs={{0,3},{1,0},{2,1},{3,2},{4,7},{5,4},{6,5},{7,6},{8,11},{9,8},{10,9... | collective-permute-start | bytes 3145736 | tf_op jit(solution)/shard_map/ppermute | solution.py:22
  75.3 10.0 %collective-permute-start.9 = (bf16[48,2048]{1,0:T(8,128)(2,1)S(1)}, bf16[48,2048]{1,0:T(8,128)(2,1)S(1)}, u32[]{:S(2)}, u32[]{:S(2)}) collective-permute-start(bf16[48,2048]{1,0:T(8,128)(2,1)S(1)} %slice.162), channel_id=1, source_target_pairs={{0,32},{32,64},{64,96},{96,128},{128,160},{160,192},{192,224},{224... | collective-permute-start | bytes 589832 | tf_op jit(solution)/shard_map/ppermute | solution.py:22
  77.2 45.4 %collective-permute-start.12 = (bf16[2048,256]{1,0:T(8,128)(2,1)S(1)}, bf16[2048,256]{1,0:T(8,128)(2,1)S(1)}, u32[]{:S(2)}, u32[]{:S(2)}) collective-permute-start(bf16[2048,256]{1,0:T(8,128)(2,1)S(1)} %get-tuple-element.39.refs_10_), channel_id=1, source_target_pairs={{0,1},{1,2},{2,3},{3,0},{4,5},{5,6},{6,7},{7,4},{8,9},{9,10},{10,1... | collective-permute-start | bytes 3145736 | tf_op jit(solution)/shard_map/ppermute | solution.py:22
  78.7 54.2 %collective-permute-start.17 = (bf16[2048,256]{1,0:T(8,128)(2,1)S(1)}, bf16[2048,256]{1,0:T(8,128)(2,1)S(1)}, u32[]{:S(2)}, u32[]{:S(2)}) collective-permute-start(bf16[2048,256]{1,0:T(8,128)(2,1)S(1)} %collective-permute-done.11.refs_0_), channel_id=1, source_target_pairs={{0,1},{1,2},{2,3},{3,0},{4,5},{5,6},{6,7},{7,4},{8,9},{9,10},{10,1... | collective-permute-start | bytes 3145736 | tf_op jit(solution)/shard_map/ppermute | solution.py:22
  85.3 62.2 %collective-permute-start.18 = (bf16[2048,256]{1,0:T(8,128)(2,1)S(1)}, bf16[2048,256]{1,0:T(8,128)(2,1)S(1)}, u32[]{:S(2)}, u32[]{:S(2)}) collective-permute-start(bf16[2048,256]{1,0:T(8,128)(2,1)S(1)} %collective-permute-done.15.refs_4_), channel_id=1, source_target_pairs={{0,3},{1,0},{2,1},{3,2},{4,7},{5,4},{6,5},{7,6},{8,11},{9,8},{10,9... | collective-permute-start | bytes 3145736 | tf_op jit(solution)/shard_map/ppermute | solution.py:22
  99.9 35.5 %collective-permute-start.19 = (bf16[1024,256]{1,0:T(8,128)(2,1)S(1)}, bf16[1024,256]{1,0:T(8,128)(2,1)S(1)}, u32[]{:S(2)}, u32[]{:S(2)}) collective-permute-start(bf16[1024,256]{1,0:T(8,128)(2,1)S(1)} %slice.140), channel_id=1, source_target_pairs={{0,1},{1,2},{2,3},{3,0},{4,5},{5,6},{6,7},{7,4},{8,9},{9,10},{10,1... | collective-permute-start | bytes 1572872 | tf_op jit(solution)/shard_map/ppermute | solution.py:22
  116.3 31.2 %collective-permute-start.20 = (bf16[1024,256]{1,0:T(8,128)(2,1)S(1)}, bf16[1024,256]{1,0:T(8,128)(2,1)S(1)}, u32[]{:S(2)}, u32[]{:S(2)}) collective-permute-start(bf16[1024,256]{1,0:T(8,128)(2,1)S(1)} %slice.141), channel_id=1, source_target_pairs={{0,3},{1,0},{2,1},{3,2},{4,7},{5,4},{6,5},{7,6},{8,11},{9,8},{10,9... | collective-permute-start | bytes 1572872 | tf_op jit(solution)/shard_map/ppermute | solution.py:22
  163.3 8.2 %collective-permute-start.23 = (f16[80,2048]{1,0:T(8,128)(2,1)S(1)}, f16[80,2048]{1,0:T(8,128)(2,1)S(1)}, u32[]{:S(2)}, u32[]{:S(2)}) collective-permute-start(f16[80,2048]{1,0:T(8,128)(2,1)S(1)} %pad_maximum_fusion.1), channel_id=1, source_target_pairs={{0,224},{32,0},{64,32},{96,64},{128,96},{160,128},{192,160},{224,1... | collective-permute-start | bytes 983048 | tf_op jit(solution)/shard_map/ppermute | solution.py:22
  163.4 9.4 %collective-permute-start.24 = (f16[80,2048]{1,0:T(8,128)(2,1)S(1)}, f16[80,2048]{1,0:T(8,128)(2,1)S(1)}, u32[]{:S(2)}, u32[]{:S(2)}) collective-permute-start(f16[80,2048]{1,0:T(8,128)(2,1)S(1)} %pad_maximum_fusion.2), channel_id=1, source_target_pairs={{0,32},{32,64},{64,96},{96,128},{128,160},{160,192},{192,224},{224... | collective-permute-start | bytes 983048 | tf_op jit(solution)/shard_map/ppermute | solution.py:22
  173.0 8.2 %collective-permute-start.25 = (f16[80,2048]{1,0:T(8,128)(2,1)S(1)}, f16[80,2048]{1,0:T(8,128)(2,1)S(1)}, u32[]{:S(2)}, u32[]{:S(2)}) collective-permute-start(f16[80,2048]{1,0:T(8,128)(2,1)S(1)} %add_convert_fusion.3), channel_id=1, source_target_pairs={{0,224},{32,0},{64,32},{96,64},{128,96},{160,128},{192,160},{224,1... | collective-permute-start | bytes 983048 | tf_op jit(solution)/shard_map/ppermute | solution.py:22
  173.1 9.5 %collective-permute-start.26 = (f16[80,2048]{1,0:T(8,128)(2,1)S(1)}, f16[80,2048]{1,0:T(8,128)(2,1)}, u32[]{:S(2)}, u32[]{:S(2)}) collective-permute-start(f16[80,2048]{1,0:T(8,128)(2,1)S(1)} %add_convert_fusion.2), channel_id=1, source_target_pairs={{0,32},{32,64},{64,96},{96,128},{128,160},{160,192},{192,224},{224... | collective-permute-start | bytes 983048 | tf_op jit(solution)/shard_map/ppermute | solution.py:22
  186.1 8.3 %collective-permute-start.28 = (f16[80,2048]{1,0:T(8,128)(2,1)S(1)}, f16[80,2048]{1,0:T(8,128)(2,1)S(1)}, u32[]{:S(2)}, u32[]{:S(2)}) collective-permute-start(f16[80,2048]{1,0:T(8,128)(2,1)S(1)} %get-tuple-element.65), channel_id=1, source_target_pairs={{0,32},{32,64},{64,96},{96,128},{128,160},{160,192},{192,224},{224... | collective-permute-start | bytes 983048 | tf_op jit(solution)/shard_map/ppermute | solution.py:22
  203.7 12.9 %all-to-all-start.1 = ((bf16[8,40,512]{2,1,0:T(8,128)(2,1)}), bf16[8,40,512]{2,1,0:T(8,128)(2,1)S(1)}, u32[]{:S(2)}, u32[]{:S(2)}) async-start(bf16[8,40,512]{2,1,0:T(8,128)(2,1)} %bitcast.30), calls=%async_computation.1 | async-start | bytes 655360 | tf_op jit(solution)/shard_map/all_to_all | solution.py:338
  (19 other events, 181.7 us)
where the time goes:
time: 244 us; the launch traced here: 242 us
  waiting for transfers between devices  109 us (45%)
  starting transfers between devices  62.1 us (25%)
  Pallas kernels  25.1 us (10%)
  blocking collectives  19.7 us (8%)
  other arithmetic  15.1 us (6%)
  between operations  4.77 us (2%)
  local copies, waits for them, and re-layouts  3.12 us (1%)
  matrix products  2.49 us (1%)
    ppermute x32, waiting for transfers between devices, shifted(): lax.ppermute(array, axis, [(i, (i + step) % count) for i in range(count)])  101 us
    ppermute x32, starting transfers between devices, shifted(): lax.ppermute(array, axis, [(i, (i + step) % count) for i in range(count)])  52.9 us
    pallas_call x3, Pallas kernels, expert_call(): pl.pallas_call(kernel, out_shape=out_shape, in_specs=[pl.BlockSpec(memory...  21.1 us
    all_to_all x1, blocking collectives, to_all(): lax.all_to_all(copies, axes, split_axis=0, concat_axis=0, tiled=True)  19.7 us
    all_to_all x1, waiting for transfers between devices, per_device(): lax.all_to_all(expert_out, EXPERT, split_axis=0, concat_axis=0, tiled=True)  8.18 us
  transfers between devices with their start and end apart: 34, of which 24 were waited for; matrix products, arithmetic and copies ran while one was open for 4% of the time, Pallas kernels for 6%

commit v1 on v0

--- a/solution.py
+++ b/solution.py
@@ -88,14 +88,23 @@
     pass_through(slots, before, total, sets)
 
 
-def last_kernel(slots, before, gate, up, low, high, *outs):
-    height, width = slots.shape
+def hidden_kernel(slots, gate, up, out):
+    chunk = slots.shape[0] // 2
+
+    @pl.loop(0, 2)
+    def _(turn):
+        rows = pl.ds(pl.multiple_of(turn * chunk, chunk), chunk)
+        out[rows, :] = hidden_of(slots, rows, [(gate, up, None)])[0]
+
+
+def last_kernel(values, before, low, high, *outs):
+    height, width = before.shape
     chunk = height // 2
     span = 512
-    weights = [(gate, up, (low, high))]
+    weights = [(None, None, (low, high))]
     for turn in (1, 0):
         rows = slice(turn * chunk, (turn + 1) * chunk)
-        hidden = hidden_of(slots, rows, weights)
+        hidden = [values[rows, :]]
         for start in range(0, width, span):
             cut = slice(start, start + span)
             value = output_of(before[rows, cut], hidden, weights, width, start, span)
@@ -299,11 +308,15 @@
         total_shape, all_rows, width, 2 * own_hidden, 0,
     )
     heights = [rows] * (dp_count - 1) + [part, part]
+    hidden = expert_call(
+        hidden_kernel, (every, gate_far, up_far),
+        jax.ShapeDtypeStruct((all_rows, own_hidden), BF16), all_rows, width, 2 * own_hidden // 3, 0,
+    )
     outs = expert_call(
         last_kernel,
-        (every, sums, gate_far, up_far, *down_far),
+        (hidden, sums, *down_far),
         [jax.ShapeDtypeStruct((height, width), F32) for height in heights],
-        all_rows, width, own_hidden, 0,
+        all_rows, width, own_hidden // 3, 0,
     )
     outs = [out * to_wire for out in outs]
 

time: 244 us -> 237 us (0.971)
  waiting for transfers between devices: 109 us -> 104 us
    ppermute x32, waiting for transfers between devices: 101 us -> 95.8 us  [shifted(): lax.ppermute(array, axis, [(i, (i + step) % count) for i in range(count)])]
    pallas_call x3 -> x4, Pallas kernels: 21.1 us -> 19.6 us  [expert_call(): pl.pallas_call(kernel, out_shape=out_shape, in_specs=[pl.BlockSpec(memory...]
  transfers between devices with their start and end apart: 34 -> 34, of which waited for: 24 -> 20; matrix products, arithmetic and copies ran while one was open for 4% -> 6% of each run, Pallas kernels for 6% -> 7%
where the time goes in v1:
time: 237 us; the launch traced here: 234 us
  waiting for transfers between devices  104 us (44%)
  starting transfers between devices  61.1 us (26%)
  Pallas kernels  23.6 us (10%)
  blocking collectives  19.4 us (8%)
  other arithmetic  15.9 us (7%)
  between operations  4.81 us (2%)
  matrix products  2.47 us (1%)
  local copies, waits for them, and re-layouts  2.38 us (1%)
    ppermute x32, waiting for transfers between devices, shifted(): lax.ppermute(array, axis, [(i, (i + step) % count) for i in range(count)])  95.8 us
    ppermute x32, starting transfers between devices, shifted(): lax.ppermute(array, axis, [(i, (i + step) % count) for i in range(count)])  52.1 us
    pallas_call x4, Pallas kernels, expert_call(): pl.pallas_call(kernel, out_shape=out_shape, in_specs=[pl.BlockSpec(memory...  19.6 us
    all_to_all x1, blocking collectives, to_all(): lax.all_to_all(copies, axes, split_axis=0, concat_axis=0, tiled=True)  19.4 us
    all_to_all x1, waiting for transfers between devices, per_device(): lax.all_to_all(expert_out, EXPERT, split_axis=0, concat_axis=0, tiled=True)  8.18 us
  transfers between devices with their start and end apart: 34, of which 20 were waited for; matrix products, arithmetic and copies ran while one was open for 6% of the time, Pallas kernels for 7%

profile of v1, /device:TPU:2, one launch (start us, length us, event | category | flops | bytes accessed | tf_op | source)
XLA Modules:
  0.0 233.7 jit_solution(5480652368528630187)
XLA Ops:
  0.7 4.0 %shard_map.113.refs_9_ = bf16[2048,256]{1,0:T(8,128)(2,1)} custom-call(f32[2]{0:T(128)} %landscape_ref.1, bf16[3,1,2048,256]{3,2,1,0:T(8,128)(2,1)} %base_ref.1, bf16[3,1,2048,256]{3,2,1,0:T(8,128)(2,1)} %one_ref.1, bf16[3,1,2048,256]{3,2,1,0:T(8,128)(2,1)} %two_ref.1, f32[2,1,256]{2,1,0:T(1,128)} %scale_ref.1), custom_call_target="tpu_custom_call" | custom-call | flops 2097152 | bytes 4194304 | tf_op jit(solution)/shard_map/pallas_call | solution.py:163
  8.4 4.5 %all-to-all-start = ((bf16[8,40,512]{2,1,0:T(8,128)(2,1)}), bf16[8,40,512]{2,1,0:T(8,128)(2,1)S(1)}, u32[]{:S(2)}, u32[]{:S(2)}) async-start(bf16[8,40,512]{2,1,0:T(8,128)(2,1)} %bitcast.7), calls=%async_computation | async-start | bytes 655360 | tf_op jit(solution)/shard_map/all_to_all | solution.py:226
  15.2 4.0 %multiply_reduce_fusion.1 = (f32[256]{0:T(256)S(1)}, bf16[2048,256]{1,0:T(8,128)(2,1)S(1)}, f32[2048]{0:T(1024)S(1)}, bf16[2048,256]{1,0:T(8,128)(2,1)}) fusion(bf16[3,1,2048,256]{3,2,1,0:T(8,128)(2,1)} %two_ref.1, f32[256]{0:T(256)S(1)} %bitcast.76, bf16[3,1,2048,256]{3,2,1,0:T(8,128)(2,1)} %one_ref.1, f32[256]{0:T(256)S(1)} %bitcast.75, ...), kind=kLoop, calls=%fused_computation.11 | loop fusion | flops 11532032 | bytes 8399872 | tf_op jit(solution)/shard_map/reduce_sum | solution.py:241
  29.0 3.8 %collective-permute-done = bf16[88,512]{1,0:T(8,128)(2,1)S(1)} collective-permute-done((bf16[88,512]{1,0:T(8,128)(2,1)S(1)}, bf16[88,512]{1,0:T(8,128)(2,1)S(1)}, u32[]{:S(2)}, u32[]{:S(2)}) %collective-permute-start) | collective-permute-done | bytes 90144 | tf_op jit(solution)/shard_map/ppermute | solution.py:22
  35.6 4.0 %collective-permute-start.4 = (bf16[88,2048]{1,0:T(8,128)(2,1)S(1)}, bf16[88,2048]{1,0:T(8,128)(2,1)S(1)}, u32[]{:S(2)}, u32[]{:S(2)}) collective-permute-start(bf16[88,2048]{1,0:T(8,128)(2,1)S(1)} %pad_maximum_fusion.refs_0_), channel_id=1, source_target_pairs={{0,224},{32,0},{64,32},{96,64},{128,96},{160,128},{192,160},{224,1... | collective-permute-start | bytes 1081352 | tf_op jit(solution)/shard_map/ppermute | solution.py:22
  42.6 5.2 %collective-permute-done.3.refs_1_ = bf16[88,2048]{1,0:T(8,128)(2,1)S(1)} collective-permute-done((bf16[88,2048]{1,0:T(8,128)(2,1)S(1)}, bf16[88,2048]{1,0:T(8,128)(2,1)S(1)}, u32[]{:S(2)}, u32[]{:S(2)}) %collective-permute-start.3) | collective-permute-done | bytes 360480 | tf_op jit(solution)/shard_map/ppermute | solution.py:22
  53.0 6.1 %collective-permute-done.5.refs_3_ = bf16[88,2048]{1,0:T(8,128)(2,1)S(1)} collective-permute-done((bf16[88,2048]{1,0:T(8,128)(2,1)S(1)}, bf16[88,2048]{1,0:T(8,128)(2,1)S(1)}, u32[]{:S(2)}, u32[]{:S(2)}) %collective-permute-start.5) | collective-permute-done | bytes 360480 | tf_op jit(solution)/shard_map/ppermute | solution.py:22
  59.1 3.2 %collective-permute-start.8 = (bf16[88,2048]{1,0:T(8,128)(2,1)S(1)}, bf16[88,2048]{1,0:T(8,128)(2,1)S(1)}, u32[]{:S(2)}, u32[]{:S(2)}) collective-permute-start(bf16[88,2048]{1,0:T(8,128)(2,1)S(1)} %collective-permute-done.6.refs_4_), channel_id=1, source_target_pairs={{0,224},{32,0},{64,32},{96,64},{128,96},{160,128},{192,160},{224,1... | collective-permute-start | bytes 1081352 | tf_op jit(solution)/shard_map/ppermute | solution.py:22
  62.3 5.4 %collective-permute-done.7.refs_5_ = bf16[88,2048]{1,0:T(8,128)(2,1)S(1)} collective-permute-done((bf16[88,2048]{1,0:T(8,128)(2,1)S(1)}, bf16[88,2048]{1,0:T(8,128)(2,1)S(1)}, u32[]{:S(2)}, u32[]{:S(2)}) %collective-permute-start.7) | collective-permute-done | bytes 360480 | tf_op jit(solution)/shard_map/ppermute | solution.py:22
  74.0 16.1 %collective-permute-done.13.refs_4_ = bf16[2048,256]{1,0:T(8,128)(2,1)S(1)} collective-permute-done((bf16[2048,256]{1,0:T(8,128)(2,1)S(1)}, bf16[2048,256]{1,0:T(8,128)(2,1)S(1)}, u32[]{:S(2)}, u32[]{:S(2)}) %collective-permute-start.13) | collective-permute-done | bytes 1048608 | tf_op jit(solution)/shard_map/ppermute | solution.py:22
  95.5 5.0 %shard_map.114 = (bf16[640,2048]{1,0:T(8,128)(2,1)S(1)}, f32[640,2048]{1,0:T(8,128)}) custom-call(s32[1]{0:T(128)} %bitcast.22.index_ref, bf16[88,2048]{1,0:T(8,128)(2,1)S(1)} %pad_maximum_fusion.refs_0_, bf16[88,2048]{1,0:T(8,128)(2,1)S(1)} %collective-permute-done.3.refs_1_, bf16[88,2048]{1,0:T(8,128)(2,1)S(1)} %collective-permute-done.4.refs_2_, ...), custom_call_target="tpu_custom_call" | custom-call | flops 2013265920 | bytes 13631488 | tf_op jit(solution)/shard_map/pallas_call | solution.py:123
  100.5 12.0 %collective-permute-done.17.refs_3_ = bf16[2048,256]{1,0:T(8,128)(2,1)S(1)} collective-permute-done((bf16[2048,256]{1,0:T(8,128)(2,1)S(1)}, bf16[2048,256]{1,0:T(8,128)(2,1)S(1)}, u32[]{:S(2)}, u32[]{:S(2)}) %collective-permute-start.17) | collective-permute-done | bytes 1048608 | tf_op jit(solution)/shard_map/ppermute | solution.py:22
  117.1 9.4 %shard_map.116.before = f32[640,2048]{1,0:T(8,128)} custom-call(bf16[640,2048]{1,0:T(8,128)(2,1)S(1)} %get-tuple-element.37.slots, f32[640,2048]{1,0:T(8,128)} %get-tuple-element.39.before, bf16[2048,256]{1,0:T(8,128)(2,1)S(1)} %collective-permute-done.11.refs_0_, bf16[2048,256]{1,0:T(8,128)(2,1)S(1)} %collective-permute-done.15.refs_1_, ...), custom_call_target="tpu_custom_call" | custom-call | flops 4026531840 | bytes 16777216 | tf_op jit(solution)/shard_map/pallas_call | solution.py:123
  126.4 8.6 %collective-permute-done.14.up = bf16[2048,256]{1,0:T(8,128)(2,1)S(1)} collective-permute-done((bf16[2048,256]{1,0:T(8,128)(2,1)S(1)}, bf16[2048,256]{1,0:T(8,128)(2,1)S(1)}, u32[]{:S(2)}, u32[]{:S(2)}) %collective-permute-start.14) | collective-permute-done | bytes 1048608 | tf_op jit(solution)/shard_map/ppermute | solution.py:22
  136.7 6.7 %collective-permute-done.20.high = bf16[1024,256]{1,0:T(8,128)(2,1)S(1)} collective-permute-done((bf16[1024,256]{1,0:T(8,128)(2,1)S(1)}, bf16[1024,256]{1,0:T(8,128)(2,1)S(1)}, u32[]{:S(2)}, u32[]{:S(2)}) %collective-permute-start.20) | collective-permute-done | bytes 524320 | tf_op jit(solution)/shard_map/ppermute | solution.py:22
  143.4 3.5 %shard_map.117 = (f32[80,2048]{1,0:T(8,128)S(1)}, f32[80,2048]{1,0:T(8,128)S(1)}, f32[80,2048]{1,0:T(8,128)S(1)}, f32[80,2048]{1,0:T(8,128)S(1)}, f32[80,2048]{1...) custom-call(bf16[640,256]{1,0:T(8,128)(2,1)S(1)} %shard_map.115.valu, ...), custom_call_target="tpu_custom_call" | custom-call | flops 668467200 | bytes 11530240 | tf_op jit(solution)/shard_map/pallas_call | solution.py:123
  149.2 3.2 %collective-permute-done.21 = f16[40,2048]{1,0:T(8,128)(2,1)S(1)} collective-permute-done((f16[40,2048]{1,0:T(8,128)(2,1)S(1)}, f16[40,2048]{1,0:T(8,128)(2,1)S(1)}, u32[]{:S(2)}, u32[]{:S(2)}) %collective-permute-start.21) | collective-permute-done | bytes 163872 | tf_op jit(solution)/shard_map/ppermute | solution.py:22
  157.9 6.4 %collective-permute-done.23 = f16[80,2048]{1,0:T(8,128)(2,1)S(1)} collective-permute-done((f16[80,2048]{1,0:T(8,128)(2,1)S(1)}, f16[80,2048]{1,0:T(8,128)(2,1)S(1)}, u32[]{:S(2)}, u32[]{:S(2)}) %collective-permute-start.23) | collective-permute-done | bytes 327712 | tf_op jit(solution)/shard_map/ppermute | solution.py:22
  168.0 6.5 %collective-permute-done.25 = f16[80,2048]{1,0:T(8,128)(2,1)S(1)} collective-permute-done((f16[80,2048]{1,0:T(8,128)(2,1)S(1)}, f16[80,2048]{1,0:T(8,128)(2,1)S(1)}, u32[]{:S(2)}, u32[]{:S(2)}) %collective-permute-start.25) | collective-permute-done | bytes 327712 | tf_op jit(solution)/shard_map/ppermute | solution.py:22
  179.2 5.0 %collective-permute-done.27 = f16[80,2048]{1,0:T(8,128)(2,1)S(1)} collective-permute-done((f16[80,2048]{1,0:T(8,128)(2,1)S(1)}, f16[80,2048]{1,0:T(8,128)(2,1)S(1)}, u32[]{:S(2)}, u32[]{:S(2)}) %collective-permute-start.27) | collective-permute-done | bytes 327712 | tf_op jit(solution)/shard_map/ppermute | solution.py:22
  186.5 4.6 %collective-permute-start.29 = (bf16[80,512]{1,0:T(8,128)(2,1)S(1)}, bf16[80,512]{1,0:T(8,128)(2,1)S(1)}, u32[]{:S(2)}, u32[]{:S(2)}) collective-permute-start(bf16[80,512]{1,0:T(8,128)(2,1)S(1)} %get-tuple-element.88), channel_id=1, source_target_pairs={{0,2},{1,3},{2,0},{3,1},{4,6},{5,7},{6,4},{7,5},{8,10},{9,11},{10,... | collective-permute-start | bytes 245768 | tf_op jit(solution)/shard_map/ppermute | solution.py:22
  196.5 4.5 %all-to-all-start.1 = ((bf16[8,40,512]{2,1,0:T(8,128)(2,1)}), bf16[8,40,512]{2,1,0:T(8,128)(2,1)S(1)}, u32[]{:S(2)}, u32[]{:S(2)}) async-start(bf16[8,40,512]{2,1,0:T(8,128)(2,1)} %bitcast.30), calls=%async_computation.1 | async-start | bytes 655360 | tf_op jit(solution)/shard_map/all_to_all | solution.py:351
  201.0 8.2 %all-to-all-done.1 = bf16[8,40,512]{2,1,0:T(8,128)(2,1)S(1)} async-done(((bf16[8,40,512]{2,1,0:T(8,128)(2,1)}), bf16[8,40,512]{2,1,0:T(8,128)(2,1)S(1)}, u32[]{:S(2)}, u32[]{:S(2)}) %all-to-all-start.1) | async-done | bytes 327712 | tf_op jit(solution)/shard_map/all_to_all | solution.py:351
  211.7 19.4 %all_to_all.15 = f32[256,1,1]{2,1,0:T(1,128)S(1)} all-to-all(f32[256,1,1]{2,1,0:T(1,128)S(1)} %broadcast_in_dim.33), channel_id=1, replica_groups=mesh['dp'=8,'expert_0'=4,'expert_1'=2,'mp'=4] {'dp','expert_0','expert_1..., dimensions={0} | all-to-all | bytes 2048 | tf_op jit(solution)/shard_map/all_to_all | solution.py:28
  (125 shorter events, 69.6 us)
Async XLA Ops:
  4.7 45.0 %collective-permute-start.11 = (bf16[2048,256]{1,0:T(8,128)(2,1)}, bf16[2048,256]{1,0:T(8,128)(2,1)S(1)}, u32[]{:S(2)}, u32[]{:S(2)}) collective-permute-start(bf16[2048,256]{1,0:T(8,128)(2,1)} %shard_map.113.refs_9_), channel_id=1, source_target_pairs={{0,1},{1,2},{2,3},{3,0},{4,5},{5,6},{6,7},{7,4},{8,9},{9,10},{10,1... | collective-permute-start | bytes 3145736 | tf_op jit(solution)/shard_map/ppermute | solution.py:22
  8.4 13.2 %all-to-all-start = ((bf16[8,40,512]{2,1,0:T(8,128)(2,1)}), bf16[8,40,512]{2,1,0:T(8,128)(2,1)S(1)}, u32[]{:S(2)}, u32[]{:S(2)}) async-start(bf16[8,40,512]{2,1,0:T(8,128)(2,1)} %bitcast.7), calls=%async_computation | async-start | bytes 655360 | tf_op jit(solution)/shard_map/all_to_all | solution.py:226
  33.6 14.1 %collective-permute-start.3 = (bf16[88,2048]{1,0:T(8,128)(2,1)S(1)}, bf16[88,2048]{1,0:T(8,128)(2,1)S(1)}, u32[]{:S(2)}, u32[]{:S(2)}) collective-permute-start(bf16[88,2048]{1,0:T(8,128)(2,1)S(1)} %pad_maximum_fusion.refs_0_), channel_id=1, source_target_pairs={{0,32},{32,64},{64,96},{96,128},{128,160},{160,192},{192,224},{224... | collective-permute-start | bytes 1081352 | tf_op jit(solution)/shard_map/ppermute | solution.py:22
  35.6 14.2 %collective-permute-start.4 = (bf16[88,2048]{1,0:T(8,128)(2,1)S(1)}, bf16[88,2048]{1,0:T(8,128)(2,1)S(1)}, u32[]{:S(2)}, u32[]{:S(2)}) collective-permute-start(bf16[88,2048]{1,0:T(8,128)(2,1)S(1)} %pad_maximum_fusion.refs_0_), channel_id=1, source_target_pairs={{0,224},{32,0},{64,32},{96,64},{128,96},{160,128},{192,160},{224,1... | collective-permute-start | bytes 1081352 | tf_op jit(solution)/shard_map/ppermute | solution.py:22
  39.6 30.9 %collective-permute-start.16 = (bf16[2048,256]{1,0:T(8,128)(2,1)}, bf16[2048,256]{1,0:T(8,128)(2,1)S(1)}, u32[]{:S(2)}, u32[]{:S(2)}) collective-permute-start(bf16[2048,256]{1,0:T(8,128)(2,1)} %get-tuple-element.40.refs_11_), channel_id=1, source_target_pairs={{0,1},{1,2},{2,3},{3,0},{4,5},{5,6},{6,7},{7,4},{8,9},{9,10},{10,1... | collective-permute-start | bytes 3145736 | tf_op jit(solution)/shard_map/ppermute | solution.py:22
  41.3 29.4 %collective-permute-start.18 = (bf16[2048,256]{1,0:T(8,128)(2,1)}, bf16[2048,256]{1,0:T(8,128)(2,1)S(1)}, u32[]{:S(2)}, u32[]{:S(2)}) collective-permute-start(bf16[2048,256]{1,0:T(8,128)(2,1)} %get-tuple-element.40.refs_11_), channel_id=1, source_target_pairs={{0,3},{1,0},{2,1},{3,2},{4,7},{5,4},{6,5},{7,6},{8,11},{9,8},{10,9... | collective-permute-start | bytes 3145736 | tf_op jit(solution)/shard_map/ppermute | solution.py:22
  47.7 42.3 %collective-permute-start.13 = (bf16[2048,256]{1,0:T(8,128)(2,1)S(1)}, bf16[2048,256]{1,0:T(8,128)(2,1)S(1)}, u32[]{:S(2)}, u32[]{:S(2)}) collective-permute-start(bf16[2048,256]{1,0:T(8,128)(2,1)S(1)} %get-tuple-element.38.refs_10_), channel_id=1, source_target_pairs={{0,3},{1,0},{2,1},{3,2},{4,7},{5,4},{6,5},{7,6},{8,11},{9,8},{10,9... | collective-permute-start | bytes 3145736 | tf_op jit(solution)/shard_map/ppermute | solution.py:22
  49.7 9.4 %collective-permute-start.5 = (bf16[88,2048]{1,0:T(8,128)(2,1)S(1)}, bf16[88,2048]{1,0:T(8,128)(2,1)S(1)}, u32[]{:S(2)}, u32[]{:S(2)}) collective-permute-start(bf16[88,2048]{1,0:T(8,128)(2,1)S(1)} %collective-permute-done.3.refs_1_), channel_id=1, source_target_pairs={{0,32},{32,64},{64,96},{96,128},{128,160},{160,192},{192,224},{224... | collective-permute-start | bytes 1081352 | tf_op jit(solution)/shard_map/ppermute | solution.py:22
  49.7 9.4 %collective-permute-start.6 = (bf16[88,2048]{1,0:T(8,128)(2,1)S(1)}, bf16[88,2048]{1,0:T(8,128)(2,1)S(1)}, u32[]{:S(2)}, u32[]{:S(2)}) collective-permute-start(bf16[88,2048]{1,0:T(8,128)(2,1)S(1)} %collective-permute-done.4.refs_2_), channel_id=1, source_target_pairs={{0,224},{32,0},{64,32},{96,64},{128,96},{160,128},{192,160},{224,1... | collective-permute-start | bytes 1081352 | tf_op jit(solution)/shard_map/ppermute | solution.py:22
  59.1 8.6 %collective-permute-start.7 = (bf16[88,2048]{1,0:T(8,128)(2,1)S(1)}, bf16[88,2048]{1,0:T(8,128)(2,1)S(1)}, u32[]{:S(2)}, u32[]{:S(2)}) collective-permute-start(bf16[88,2048]{1,0:T(8,128)(2,1)S(1)} %collective-permute-done.5.refs_3_), channel_id=1, source_target_pairs={{0,32},{32,64},{64,96},{96,128},{128,160},{160,192},{192,224},{224... | collective-permute-start | bytes 1081352 | tf_op jit(solution)/shard_map/ppermute | solution.py:22
  59.1 11.5 %collective-permute-start.8 = (bf16[88,2048]{1,0:T(8,128)(2,1)S(1)}, bf16[88,2048]{1,0:T(8,128)(2,1)S(1)}, u32[]{:S(2)}, u32[]{:S(2)}) collective-permute-start(bf16[88,2048]{1,0:T(8,128)(2,1)S(1)} %collective-permute-done.6.refs_4_), channel_id=1, source_target_pairs={{0,224},{32,0},{64,32},{96,64},{128,96},{160,128},{192,160},{224,1... | collective-permute-start | bytes 1081352 | tf_op jit(solution)/shard_map/ppermute | solution.py:22
  67.7 44.8 %collective-permute-start.17 = (bf16[2048,256]{1,0:T(8,128)(2,1)S(1)}, bf16[2048,256]{1,0:T(8,128)(2,1)S(1)}, u32[]{:S(2)}, u32[]{:S(2)}) collective-permute-start(bf16[2048,256]{1,0:T(8,128)(2,1)S(1)} %copy-done.1), channel_id=1, source_target_pairs={{0,3},{1,0},{2,1},{3,2},{4,7},{5,4},{6,5},{7,6},{8,11},{9,8},{10,9... | collective-permute-start | bytes 3145736 | tf_op jit(solution)/shard_map/ppermute | solution.py:22
  70.5 21.5 %collective-permute-start.9 = (bf16[48,2048]{1,0:T(8,128)(2,1)S(1)}, bf16[48,2048]{1,0:T(8,128)(2,1)S(1)}, u32[]{:S(2)}, u32[]{:S(2)}) collective-permute-start(bf16[48,2048]{1,0:T(8,128)(2,1)S(1)} %slice.162), channel_id=1, source_target_pairs={{0,32},{32,64},{64,96},{96,128},{128,160},{160,192},{192,224},{224... | collective-permute-start | bytes 589832 | tf_op jit(solution)/shard_map/ppermute | solution.py:22
  70.6 46.4 %collective-permute-start.15 = (bf16[2048,256]{1,0:T(8,128)(2,1)S(1)}, bf16[2048,256]{1,0:T(8,128)(2,1)S(1)}, u32[]{:S(2)}, u32[]{:S(2)}) collective-permute-start(bf16[2048,256]{1,0:T(8,128)(2,1)S(1)} %get-tuple-element.38.refs_10_), channel_id=1, source_target_pairs={{0,1},{1,2},{2,3},{3,0},{4,5},{5,6},{6,7},{7,4},{8,9},{9,10},{10,1... | collective-permute-start | bytes 3145736 | tf_op jit(solution)/shard_map/ppermute | solution.py:22
  70.8 21.1 %collective-permute-start.10 = (bf16[40,2048]{1,0:T(8,128)(2,1)S(1)}, bf16[40,2048]{1,0:T(8,128)(2,1)S(1)}, u32[]{:S(2)}, u32[]{:S(2)}) collective-permute-start(bf16[40,2048]{1,0:T(8,128)(2,1)S(1)} %slice.163), channel_id=1, source_target_pairs={{0,224},{32,0},{64,32},{96,64},{128,96},{160,128},{192,160},{224,1... | collective-permute-start | bytes 491528 | tf_op jit(solution)/shard_map/ppermute | solution.py:22
  90.0 36.4 %collective-permute-start.12 = (bf16[2048,256]{1,0:T(8,128)(2,1)S(1)}, bf16[2048,256]{1,0:T(8,128)(2,1)S(1)}, u32[]{:S(2)}, u32[]{:S(2)}) collective-permute-start(bf16[2048,256]{1,0:T(8,128)(2,1)S(1)} %collective-permute-done.11.refs_0_), channel_id=1, source_target_pairs={{0,1},{1,2},{2,3},{3,0},{4,5},{5,6},{6,7},{7,4},{8,9},{9,10},{10,1... | collective-permute-start | bytes 3145736 | tf_op jit(solution)/shard_map/ppermute | solution.py:22
  91.9 43.1 %collective-permute-start.14 = (bf16[2048,256]{1,0:T(8,128)(2,1)S(1)}, bf16[2048,256]{1,0:T(8,128)(2,1)S(1)}, u32[]{:S(2)}, u32[]{:S(2)}) collective-permute-start(bf16[2048,256]{1,0:T(8,128)(2,1)S(1)} %collective-permute-done.13.refs_4_), channel_id=1, source_target_pairs={{0,3},{1,0},{2,1},{3,2},{4,7},{5,4},{6,5},{7,6},{8,11},{9,8},{10,9... | collective-permute-start | bytes 3145736 | tf_op jit(solution)/shard_map/ppermute | solution.py:22
  92.1 44.6 %collective-permute-start.19 = (bf16[1024,256]{1,0:T(8,128)(2,1)S(1)}, bf16[1024,256]{1,0:T(8,128)(2,1)S(1)}, u32[]{:S(2)}, u32[]{:S(2)}) collective-permute-start(bf16[1024,256]{1,0:T(8,128)(2,1)S(1)} %slice.140), channel_id=1, source_target_pairs={{0,1},{1,2},{2,3},{3,0},{4,5},{5,6},{6,7},{7,4},{8,9},{9,10},{10,1... | collective-permute-start | bytes 1572872 | tf_op jit(solution)/shard_map/ppermute | solution.py:22
  112.5 30.9 %collective-permute-start.20 = (bf16[1024,256]{1,0:T(8,128)(2,1)S(1)}, bf16[1024,256]{1,0:T(8,128)(2,1)S(1)}, u32[]{:S(2)}, u32[]{:S(2)}) collective-permute-start(bf16[1024,256]{1,0:T(8,128)(2,1)S(1)} %slice.141), channel_id=1, source_target_pairs={{0,3},{1,0},{2,1},{3,2},{4,7},{5,4},{6,5},{7,6},{8,11},{9,8},{10,9... | collective-permute-start | bytes 1572872 | tf_op jit(solution)/shard_map/ppermute | solution.py:22
  155.6 8.8 %collective-permute-start.23 = (f16[80,2048]{1,0:T(8,128)(2,1)S(1)}, f16[80,2048]{1,0:T(8,128)(2,1)S(1)}, u32[]{:S(2)}, u32[]{:S(2)}) collective-permute-start(f16[80,2048]{1,0:T(8,128)(2,1)S(1)} %pad_maximum_fusion.1), channel_id=1, source_target_pairs={{0,224},{32,0},{64,32},{96,64},{128,96},{160,128},{192,160},{224,1... | collective-permute-start | bytes 983048 | tf_op jit(solution)/shard_map/ppermute | solution.py:22
  155.9 9.8 %collective-permute-start.24 = (f16[80,2048]{1,0:T(8,128)(2,1)S(1)}, f16[80,2048]{1,0:T(8,128)(2,1)S(1)}, u32[]{:S(2)}, u32[]{:S(2)}) collective-permute-start(f16[80,2048]{1,0:T(8,128)(2,1)S(1)} %pad_maximum_fusion.2), channel_id=1, source_target_pairs={{0,32},{32,64},{64,96},{96,128},{128,160},{160,192},{192,224},{224... | collective-permute-start | bytes 983048 | tf_op jit(solution)/shard_map/ppermute | solution.py:22
  165.9 8.6 %collective-permute-start.25 = (f16[80,2048]{1,0:T(8,128)(2,1)S(1)}, f16[80,2048]{1,0:T(8,128)(2,1)S(1)}, u32[]{:S(2)}, u32[]{:S(2)}) collective-permute-start(f16[80,2048]{1,0:T(8,128)(2,1)S(1)} %add_convert_fusion.3), channel_id=1, source_target_pairs={{0,224},{32,0},{64,32},{96,64},{128,96},{160,128},{192,160},{224,1... | collective-permute-start | bytes 983048 | tf_op jit(solution)/shard_map/ppermute | solution.py:22
  165.9 9.9 %collective-permute-start.26 = (f16[80,2048]{1,0:T(8,128)(2,1)S(1)}, f16[80,2048]{1,0:T(8,128)(2,1)}, u32[]{:S(2)}, u32[]{:S(2)}) collective-permute-start(f16[80,2048]{1,0:T(8,128)(2,1)S(1)} %add_convert_fusion.2), channel_id=1, source_target_pairs={{0,32},{32,64},{64,96},{96,128},{128,160},{160,192},{192,224},{224... | collective-permute-start | bytes 983048 | tf_op jit(solution)/shard_map/ppermute | solution.py:22
  196.5 12.7 %all-to-all-start.1 = ((bf16[8,40,512]{2,1,0:T(8,128)(2,1)}), bf16[8,40,512]{2,1,0:T(8,128)(2,1)S(1)}, u32[]{:S(2)}, u32[]{:S(2)}) async-start(bf16[8,40,512]{2,1,0:T(8,128)(2,1)} %bitcast.30), calls=%async_computation.1 | async-start | bytes 655360 | tf_op jit(solution)/shard_map/all_to_all | solution.py:351
  (20 other events, 267.5 us)
